TPU v7x, 256 devices: a whole 4x4x8 slice. The times are simulated.
256 devices in a mesh: seg: 32 (over z, y), op: 8 (over x, core).
Axes of the slice: x: 4, y: 4, z: 8, core: 2. Of those that a mesh axis runs over, the one named last changes fastest.
Arguments:
- label_map: int32 [32, 16], P('seg'), may hold values from 0 to 15, each once within a row
- site_blocks: float32 [32, 16, 128, 128], P('seg'), may hold values from -0.25 to 1.25
- left_ops: bfloat16 [96, 16, 128, 128], P('op'), may hold values from -0.5 to 0.5
- right_ops: bfloat16 [32, 96, 16, 128, 128], P('seg', 'op'), may hold values from -0.0546875 to 0.0546875
- wavefunction: bfloat16 [32, 16, 128, 128], P('seg', 'op'), may hold values from -72 to 72
Outputs:
- ham_psi: bfloat16 [32, 16, 128, 128], P('seg', 'op')
- ham_squared_psi: bfloat16 [32, 16, 128, 128], P('seg', 'op')
Inputs may be any that keep to these rules, and one draw needn't show every extreme that they name: Each row of label_map is a permutation of 0 to 15.
All inputs are finite; a program needn't handle non-finite values.
Results may differ from a plain program's by a relative error of at most 0.022.
Values may be sent and summed in bfloat16 or wider, within the bound.
No kernel may reach another device: no remote copies, remote signals or barrier semaphores. Data moves between devices by JAX's collectives and lax.ppermute only.
A program may use at most 128 MiB of HBM per device.

v0:
```python
import jax
import jax.numpy as jnp
from jax import lax
from jax.sharding import Mesh
from jax.sharding import PartitionSpec as P

SEG = ("seg_0", "seg_1")


def neutral_like(array, identity):
    return jax.tree.map(
        lambda part, zero: jnp.zeros_like(part) + jnp.asarray(zero, part.dtype), array, identity
    )


def prefix_by_axis(array, axes, combine, identity):
    before = start = neutral_like(array, identity)
    running = array
    for axis in reversed(axes):
        peers, index = (lax.axis_size(axis), lax.axis_index(axis))
        pieces = jax.tree.map(lambda part: lax.all_gather(part, axis), running)
        inside, running = (start, start)
        for k in range(peers):
            passed = k < index
            running = combine(running, jax.tree.map(lambda part: part[k], pieces))
            inside = jax.tree.map(lambda new, old: jnp.where(passed, new, old), running, inside)
        before = combine(inside, before)
    return before


def sent_to_all(array, axis):
    peers = lax.axis_size(axis)
    return lax.all_to_all(
        jnp.broadcast_to(array[None], (peers, *array.shape)), axis, 0, 0, tiled=True
    )


def laid_out(tiles, dim):
    tiles = jnp.moveaxis(tiles, 0, dim)
    lengths = tiles.shape
    return tiles.reshape(*lengths[:dim], lengths[dim] * lengths[dim + 1], *lengths[dim + 2 :])


def collect(array, axis, dim):
    tiles = sent_to_all(array, axis)
    return laid_out(tiles, dim)


def split_up(array, dim, peers):
    lengths = array.shape
    tiles = array.reshape(*lengths[:dim], peers, lengths[dim] // peers, *lengths[dim + 1 :])
    return jnp.moveaxis(tiles, dim, 0)


def sum_at_owner(array, axis, dim):
    peers = lax.axis_size(axis)
    tiles = lax.all_to_all(split_up(array, dim, peers), axis, 0, 0, tiled=True)
    return jnp.sum(tiles.astype(jnp.float32), axis=0)


def of_everyone(array, axis):
    return sent_to_all(array, axis).sum(axis=0)


def on_device(label_map, site_blocks, left_ops, right_ops, wavefunction):
    highest = lax.Precision.HIGHEST
    sectors = site_blocks.shape[1]
    block_len = site_blocks.shape[2]
    sector_map = label_map[0]
    own_blocks = site_blocks[0]
    identity = jnp.eye(block_len, dtype=jnp.float32)

    def compose(former, latter):
        position = former[1].astype(jnp.int32)
        joined = jnp.einsum(
            "qij,qjk->qik", former[0], jnp.take(latter[0], position, axis=0), precision=highest
        )
        return (joined, jnp.take(latter[1], position))

    neutral = (
        jnp.broadcast_to(identity, (sectors, block_len, block_len)),
        jnp.arange(sectors, dtype=jnp.float32),
    )
    prefix, prefix_labels = prefix_by_axis(
        (own_blocks, sector_map.astype(jnp.float32)), SEG, compose, neutral
    )
    labels_int = prefix_labels.astype(jnp.int32)
    inverse = jnp.argsort(labels_int)
    inner_prod = jnp.einsum(
        "kqjl,qlm->kqjm", left_ops, prefix, precision=highest, preferred_element_type=jnp.float32
    )
    environ = jnp.einsum("qji,kqjm->kqim", prefix, inner_prod, precision=highest)
    environ = jnp.take(environ, inverse, axis=1).astype(jnp.bfloat16)
    right_local = right_ops[0]

    def apply_ham(portion):
        half_prod = jnp.einsum(
            "kpij,pjl->kpil", environ, portion, preferred_element_type=jnp.float32
        ).astype(jnp.bfloat16)
        return jnp.einsum(
            "kpil,kpml->pim", half_prod, right_local, preferred_element_type=jnp.float32
        )

    partial_sum = apply_ham(collect(wavefunction[0], "op", 0))
    entries = sectors * block_len * block_len
    hpsi_part = sum_at_owner(partial_sum.astype(jnp.bfloat16), "op", 0)
    norm_total = of_everyone(jnp.sum(hpsi_part * hpsi_part), "op")
    scale_fac = lax.rsqrt(norm_total / entries + 1e-06)
    unit_part = (hpsi_part * scale_fac).astype(jnp.bfloat16)
    first_out = hpsi_part.astype(jnp.bfloat16)
    second_part = apply_ham(collect(unit_part, "op", 0))
    second_out = sum_at_owner(second_part.astype(jnp.bfloat16), "op", 0).astype(jnp.bfloat16)
    return (first_out[None], second_out[None])


def solution(mesh):
    split = Mesh(mesh.devices.reshape(8, 4, mesh.shape["op"]), ("seg_0", "seg_1", "op"))
    placed = (
        P(SEG, None),
        P(SEG, None, None, None),
        P("op", None, None, None),
        P(SEG, "op", None, None, None),
        P(SEG, "op", None, None),
    )
    return jax.shard_map(
        on_device,
        mesh=split,
        in_specs=placed,
        out_specs=(P(SEG, "op", None, None), P(SEG, "op", None, None)),
        check_vma=False,
    )
```

profile of v0, /device:TPU:1, one launch (start us, length us, event | category | flops | bytes accessed | tf_op | source)
XLA Modules:
  0.0 319.6 jit_solution(1148708545683901217)
XLA Ops:
  8.6 8.8 %all-gather.2 = f32[4,1,16]{2,1,0:T(1,128)S(1)} all-gather(f32[1,1,16]{2,1,0:T(1,128)S(1)} %convert_bitcast_fusion.1), channel_id=1, replica_groups=mesh['seg_0'=8,'seg_1'=4,'op'=8] {'seg_1'}, dimensions={0}, use_global_device_ids=true | all-gather | bytes 320 | tf_op jit(solution)/shard_map/all_gather | solution.py:21
  19.5 44.7 %all-gather.6.cloned.1.call-done = f32[4,16,128,128]{3,2,1,0:T(8,128)} async-done(((f32[1,16,128,128]{3,2,1,0:T(8,128)}), f32[4,16,128,128]{3,2,1,0:T(8,128)}) %all-gather.6.cloned.1.call-update) | async-done | bytes 4194320 | tf_op jit(solution)/shard_map/all_gather | solution.py:21
  64.2 3.9 %slice_bitcast_fusion = (f32[16,128,128]{2,1,0:T(8,128)S(1)}, f32[16,128,128]{2,1,0:T(8,128)}, f32[16,128,128]{2,1,0:T(8,128)S(1)}, f32[16,128,128]{2,1,0:T(8,128)}) fusion(f32[4,16,128,128]{3,2,1,0:T(8,128)} %all-gather.6.cloned.1.call-done), kind=kLoop, calls=%fused_computation.52 | loop fusion | bytes 8388608 | tf_op jit(solution)/shard_map/squeeze | solution.py:25
  68.7 1.8 gather_fusion.15
  70.6 2.8 gather_fusion.17
  77.3 2.4 fusion.60
  80.8 2.2 fusion.58
  83.9 5.1 %all-to-all-start = ((bf16[8,2,128,128]{3,2,1,0:T(8,128)(2,1)}), bf16[8,2,128,128]{3,2,1,0:T(8,128)(2,1)}, u32[]{:S(2)}, u32[]{:S(2)}) async-start(bf16[8,2,128,128]{3,2,1,0:T(8,128)(2,1)} %broadcast_in_dim.63), calls=%async_computation | async-start | bytes 1048576 | tf_op jit(solution)/shard_map/all_to_all | solution.py:33
  91.0 16.4 %all-reduce = f32[128]{0:T(128)S(1)} all-reduce(f32[128]{0:T(128)S(1)} %fusion.108), channel_id=2, replica_groups=mesh['seg_0'=8,'seg_1'=4,'op'=8] {'seg_0'}, use_global_device_ids=true, to_apply=%add | all-reduce | flops 128 | bytes 1024
  110.1 2.8 gather_fusion.27
  119.8 3.6 %fusion.41 = f32[16,128,128]{2,1,0:T(8,128)} fusion(f32[16,128,128]{2,1,0:T(8,128)} %gather_fusion.27, f32[16,128,128]{2,1,0:T(8,128)S(1)} %copy-done, f32[16,128,128]{2,1,0:T(8,128)} %copy-done.1, f32[16,128,128]{2,1,0:T(8,128)S(1)} %fusion.62, f32[16,128,128]{2,1,0:T(8,128)S(1)} %fusion.64, f32[128,128]{1,0:T(8,128)S(1)} %fusion.105, ...), kind=kOutput, calls=%fused_computation.57 | convolution fusion | flops 403963904 | bytes 6357012 | tf_op jit(solution)/shard_map/qij,qjk->qik/dot_general | solution.py:75
  123.4 2.9 gather_fusion.28
  126.3 51.6 %all-gather.8.cloned.1.call-done = f32[128,128,128]{2,1,0:T(8,128)} async-done(((f32[16,128,128]{2,1,0:T(8,128)}), f32[128,128,128]{2,1,0:T(8,128)}) %all-gather.8.cloned.1.call-update) | async-done | bytes 8388624 | tf_op jit(solution)/shard_map/all_gather | solution.py:21
  177.8 6.3 %fusion.127 = (f32[16,128,128]{2,1,0:T(8,128)}, f32[16,128,128]{2,1,0:T(8,128)S(1)}, f32[16,128,128]{2,1,0:T(8,128)}, f32[16,128,128]{2,1,0:T(8,128)}, f32[16,12...) fusion(f32[128,128,128]{2,1,0:T(8,128)} %all-gather.8.cloned.1.call-done), kind=kLoop, calls=%fused_computation.216 | loop fusion | bytes 16777216 | tf_op jit(solution)/shard_map/slice | solution.py:25
  184.1 1.8 gather_fusion.26
  187.5 2.3 fusion.56
  189.8 2.8 gather_fusion.20
  192.7 2.8 gather_fusion.21
  195.5 2.8 gather_fusion.22
  198.3 2.8 gather_fusion.23
  201.1 2.8 gather_fusion.24
  205.6 2.6 fusion.54
  208.2 2.5 fusion.52
  218.7 5.1 %fusion.7 = f32[16,128,12,128]{3,1,2,0:T(8,128)S(1)} fusion(f32[16,128,128,1]{2,1,3,0:T(8,128)S(1)} %convolution_bitcast_fusion, bf16[12,16,128,128]{3,2,1,0:T(8,128)(2,1)S(1)} %bitcast.102), kind=kOutput, calls=%fused_computation.37 | convolution fusion | flops 4831838208 | bytes 19922944 | tf_op jit(solution)/shard_map/kqjl,qlm->kqjm/dot_general | solution.py:89
  223.8 13.1 %fusion.15 = bf16[12,16,128,128]{2,3,0,1:T(8,128)(2,1)} fusion(f32[16,128,128,1]{2,1,3,0:T(8,128)S(1)} %convolution_bitcast_fusion, f32[16,128,12,128]{3,1,2,0:T(8,128)S(1)} %fusion.7), kind=kOutput, calls=%fused_computation.44 | convolution fusion | flops 4831838208 | bytes 19922944 | tf_op jit(solution)/shard_map/qji,kqjm->kqim/dot_general | solution.py:92
  236.9 6.8 %gather_fusion = bf16[16,12,128,128]{2,3,1,0:T(8,128)(2,1)} fusion(bf16[12,16,128,128]{2,3,0,1:T(8,128)(2,1)} %fusion.15, s32[1024]{0:T(1024)S(1)} %pad_clamp_fusion), kind=kCustom, calls=%fused_computation.28 | custom fusion | bytes 12582976 | tf_op jit(solution)/shard_map/jit(_take)/gather | solution.py:93
  243.7 8.7 %fusion.30 = bf16[16,128,128]{2,1,0:T(8,128)(2,1)S(1)} fusion(bf16[16,128,128,1]{2,1,3,0:T(8,128)(2,1)} %bitcast.19, bf16[16,12,128,128]{2,3,1,0:T(8,128)(2,1)} %gather_fusion, pred[16]{0:T(512)(128)(4,1)S(1)} %compare_and_fusion.13, bf16[1,12,16,128,128]{4,3,2,1,0:T(8,128)(2,1)} %param.12), kind=kOutput, calls=%fused_computation.50 | convolution fusion | flops 1617166336 | bytes 13631504 | tf_op jit(solution)/shard_map/kpil,kpml->pim/dot_general | solution.py:100
  252.4 14.2 %all_to_all.26 = bf16[8,2,128,128]{3,2,1,0:T(8,128)(2,1)S(1)} all-to-all(bf16[8,2,128,128]{3,2,1,0:T(8,128)(2,1)S(1)} %bitcast.105), channel_id=1, replica_groups=mesh['seg_0'=8,'seg_1'=4,'op'=8] {'op'}, dimensions={0} | all-to-all | bytes 1048576 | tf_op jit(solution)/shard_map/all_to_all | solution.py:57
  268.0 8.0 %all_to_all.27 = f32[8,1,1]{2,1,0:T(1,128)S(1)} all-to-all(f32[8,1,1]{2,1,0:T(1,128)S(1)} %broadcast_in_dim.64), channel_id=1, replica_groups=mesh['seg_0'=8,'seg_1'=4,'op'=8] {'op'}, dimensions={0} | all-to-all | bytes 64 | tf_op jit(solution)/shard_map/all_to_all | solution.py:33
  278.2 12.7 %all_to_all.28 = bf16[8,2,128,128]{2,3,1,0:T(8,128)(2,1)S(1)} all-to-all(bf16[8,2,128,128]{2,3,1,0:T(8,128)(2,1)S(1)} %broadcast_in_dim.65), channel_id=1, replica_groups=mesh['seg_0'=8,'seg_1'=4,'op'=8] {'op'}, dimensions={0} | all-to-all | bytes 1048576 | tf_op jit(solution)/shard_map/all_to_all | solution.py:33
  290.9 8.2 %fusion.35 = bf16[16,128,128]{2,1,0:T(8,128)(2,1)S(1)} fusion(bf16[16,128,128,1]{1,2,3,0:T(8,128)(2,1)S(1)} %bitcast.103, bf16[16,12,128,128]{2,3,1,0:T(8,128)(2,1)} %gather_fusion, pred[16]{0:T(512)(128)(4,1)S(1)} %compare_and_fusion.13, bf16[1,12,16,128,128]{4,3,2,1,0:T(8,128)(2,1)} %param.12), kind=kOutput, calls=%fused_computation.51 | convolution fusion | flops 1617166336 | bytes 13631504 | tf_op jit(solution)/shard_map/kpil,kpml->pim/dot_general | solution.py:100
  299.1 12.8 %all_to_all.29 = bf16[8,2,128,128]{3,2,1,0:T(8,128)(2,1)S(1)} all-to-all(bf16[8,2,128,128]{3,2,1,0:T(8,128)(2,1)S(1)} %bitcast.104), channel_id=1, replica_groups=mesh['seg_0'=8,'seg_1'=4,'op'=8] {'op'}, dimensions={0} | all-to-all | bytes 1048576 | tf_op jit(solution)/shard_map/all_to_all | solution.py:57
  (108 shorter events, 35.3 us)
Async XLA Ops:
  7.2 57.1 %all-gather.6.cloned.1.call-start = ((), (), s32[]{:S(2)}) async-start(), calls=%async_computation.5 | async-start | bytes 5242880 | tf_op jit(solution)/shard_map/all_gather | solution.py:21
  7.9 169.9 %all-gather.8.cloned.1.call-start = ((), (), s32[]{:S(2)}) async-start(), calls=%async_computation.6 | async-start | bytes 9437184 | tf_op jit(solution)/shard_map/all_gather | solution.py:21
  75.0 5.8 %copy-start.7 = (f32[16,128,128]{2,1,0:T(8,128)S(1)}, f32[16,128,128]{2,1,0:T(8,128)}, u32[]{:S(2)}) copy-start(f32[16,128,128]{2,1,0:T(8,128)} %gather_fusion.18) | copy-start | bytes 3145732
  75.0 8.0 %copy-start.8 = (bf16[1,2,128,128]{3,2,1,0:T(8,128)(2,1)S(1)}, bf16[1,2,128,128]{3,2,1,0:T(8,128)(2,1)}, u32[]{:S(2)}) copy-start(bf16[1,2,128,128]{3,2,1,0:T(8,128)(2,1)} %param.13) | copy-start | bytes 196612
  76.1 13.6 %copy-start.9 = (u32[256]{0:T(256)S(1)}, u32[256]{0:T(256)}, u32[]{:S(2)}) copy-start(u32[256]{0:T(256)} %constant.77) | copy-start | bytes 3076
  79.7 1.1 copy-start.1
  83.0 36.8 %copy-start = (f32[16,128,128]{2,1,0:T(8,128)S(1)}, f32[16,128,128]{2,1,0:T(8,128)}, u32[]{:S(2)}) copy-start(f32[16,128,128]{2,1,0:T(8,128)} %fusion.58) | copy-start | bytes 3145732
  83.9 159.8 %all-to-all-start = ((bf16[8,2,128,128]{3,2,1,0:T(8,128)(2,1)}), bf16[8,2,128,128]{3,2,1,0:T(8,128)(2,1)}, u32[]{:S(2)}, u32[]{:S(2)}) async-start(bf16[8,2,128,128]{3,2,1,0:T(8,128)(2,1)} %broadcast_in_dim.63), calls=%async_computation | async-start | bytes 1048576 | tf_op jit(solution)/shard_map/all_to_all | solution.py:33
  205.6 5.1 %copy-start.6 = (f32[16,128,128]{2,1,0:T(8,128)S(1)}, f32[16,128,128]{2,1,0:T(8,128)}, u32[]{:S(2)}) copy-start(f32[16,128,128]{2,1,0:T(8,128)} %gather_fusion.22) | copy-start | bytes 3145732
  205.6 6.3 %copy-start.5 = (f32[16,128,128]{2,1,0:T(8,128)S(1)}, f32[16,128,128]{2,1,0:T(8,128)}, u32[]{:S(2)}) copy-start(f32[16,128,128]{2,1,0:T(8,128)} %gather_fusion.23) | copy-start | bytes 3145732
  205.6 7.6 %copy-start.3 = (f32[16,128,128]{2,1,0:T(8,128)S(1)}, f32[16,128,128]{2,1,0:T(8,128)}, u32[]{:S(2)}) copy-start(f32[16,128,128]{2,1,0:T(8,128)} %gather_fusion.24) | copy-start | bytes 3145732
  208.2 6.2 %copy-start.4 = (f32[16,128,128]{2,1,0:T(8,128)S(1)}, f32[16,128,128]{2,1,0:T(8,128)}, u32[]{:S(2)}) copy-start(f32[16,128,128]{2,1,0:T(8,128)} %gather_fusion.25) | copy-start | bytes 3145732
  214.4 3.1 copy-start.2
  215.8 2.9 slice-start
  215.8 2.9 slice-start.1
Sparse Core Ops, SparseCore 0:
  9.8 54.3 all-gather.5
  83.1 94.6 all-gather.7
where the time goes:
time: 326 us; the launch traced here: 320 us
  waiting for transfers between devices  97 us (30%)
  blocking collectives  72.8 us (22%)
  local copies, waits for them, and re-layouts  62.6 us (19%)
  matrix products  60.8 us (19%)
  between operations  16.2 us (5%)
  starting transfers between devices  5.17 us (2%)
  other arithmetic  5.03 us (2%)
    all_gather x2, waiting for transfers between devices, prefix_by_axis(): pieces = jax.tree.map(lambda part: lax.all_gather(part, axis), running)  96.3 us
    gather x14, local copies, waits for them, and re-layouts, compose(): jnp.take(latter[0], position, axis=0)  31.7 us
    all_to_all x2, blocking collectives, sum_at_owner(): tiles = lax.all_to_all(split_up(array, dim, peers), axis, 0, 0, tiled=True)  27 us
    dot_general x14, matrix products, compose(): jnp.einsum('qij,qjk->qik', former[0], jnp.take(latter[0], position, axis=...  25.7 us
    all_to_all x2, blocking collectives, sent_to_all(): lax.all_to_all(jnp.broadcast_to(array[None], (peers, *array.shape)), axis...  20.7 us
    dot_general x2, matrix products, apply_ham(): jnp.einsum('kpil,kpml->pim', half_prod, right_local, preferred_element_ty...  16.9 us
    unnamed x1, blocking collectives  16.4 us
    dot_general x1, matrix products, on_device(): jnp.einsum('qji,kqjm->kqim', prefix, inner_prod, precision=highest)  13.1 us
  transfers between devices with their start and end apart: 3, of which 2 were waited for; matrix products, arithmetic and copies ran while one was open for 28% of the time, Pallas kernels for 0%

commit v1 on v0

v1 whole, which is shorter than its diff:
```python
import functools

import jax
import jax.numpy as jnp
from jax import lax
from jax.experimental import pallas as pl
from jax.experimental.pallas import tpu as pltpu
from jax.sharding import Mesh
from jax.sharding import PartitionSpec as P

SEG = ("z", "y")
OP = ("x", "c")
NZ, NY, NX, NC = 8, 4, 4, 2
N = 128
CODE_ROWS = N + 16
SCALE = 2.0**-27
UNSCALE = 2.0**54
HIGHEST = lax.Precision.HIGHEST
VMEM = pl.BlockSpec(memory_space=pltpu.VMEM)
SMEM = pl.BlockSpec(memory_space=pltpu.SMEM)
LN2 = 0.6931471805599453


def shift(n, d):
    return [(i, (i + d) % n) for i in range(n)]


def call(kernel, outs, specs, out_specs, args, scratch=(), flops=0, limit=None):
    return pl.pallas_call(
        kernel,
        out_shape=outs,
        in_specs=specs,
        out_specs=out_specs,
        scratch_shapes=list(scratch),
        cost_estimate=pl.CostEstimate(flops=flops, bytes_accessed=1 << 20, transcendentals=0),
        compiler_params=pltpu.CompilerParams(vmem_limit_bytes=limit),
    )(*args)


def encode(x):
    top = jnp.maximum(jnp.max(jnp.abs(x), axis=0, keepdims=True), 1e-30)
    power = jnp.ceil(jnp.log(top) * (1.0 / LN2))
    coded = jnp.round(x * (jnp.exp(power * -LN2) * 32760.0)).astype(jnp.int32)
    powers = jnp.broadcast_to(power, (16, N)).astype(jnp.int32)
    return coded.astype(jnp.int16), powers.astype(jnp.int16)


def decode(ref):
    coded = ref[0:N, :].astype(jnp.int32).astype(jnp.float32)
    power = ref[N:CODE_ROWS, :].astype(jnp.int32).astype(jnp.float32)[0:1, :]
    return coded * (jnp.exp(power * LN2) * (1.0 / 32760.0))


def mm(a, b):
    return jnp.dot(a, b, precision=HIGHEST, preferred_element_type=jnp.float32)


def select_kernel(at_ref, maps_ref, blocks_ref, code_ref, inverse_ref):
    seg = at_ref[0]
    own = at_ref[1]

    def step(s, labels):
        return tuple(maps_ref[s, label] for label in labels)

    labels = lax.fori_loop(0, seg, step, tuple(jnp.int32(q) for q in range(16)))
    for q in range(16):
        inverse_ref[labels[q]] = jnp.int32(q)
    for i in range(2):
        label = jnp.int32(0)
        for q in range(16):
            label = jnp.where(own * 2 + i == q, labels[q], label)
        coded, powers = encode(blocks_ref[label])
        code_ref[i, 0:N, :] = coded
        code_ref[i, N:CODE_ROWS, :] = powers


def row_kernel(at_ref, s0, s1, s2, s3, code_ref, before_ref, held):
    y = at_ref[2]
    for d, ref in enumerate((s0, s1, s2, s3)):
        for i in range(2):
            held[lax.rem(y - d + NY, NY), i] = decode(ref.at[i])
    diagonal = lax.broadcasted_iota(jnp.int32, (N, N), 0) == lax.broadcasted_iota(
        jnp.int32, (N, N), 1
    )
    identity = diagonal.astype(jnp.float32)
    for i in range(2):
        first = mm(held[0, i], held[1, i])
        last = mm(held[2, i], held[3, i])
        three = mm(first, held[2, i])
        coded, powers = encode(mm(first, last))
        for z in range(NZ):
            code_ref[z, i, 0:N, :] = coded
            code_ref[z, i, N:CODE_ROWS, :] = powers
        low = jnp.where(y == 0, identity, held[0, i])
        high = jnp.where(y == 2, first, three)
        before_ref[i] = jnp.where(y < 2, low, high)


def chain_kernel(at_ref, codes_ref, before_ref, psi_ref, out_ref):
    z = at_ref[3]
    diagonal = lax.broadcasted_iota(jnp.int32, (N, N), 0) == lax.broadcasted_iota(
        jnp.int32, (N, N), 1
    )
    identity = diagonal.astype(jnp.float32)
    for i in range(2):
        factors = [
            jnp.where(k < z, decode(codes_ref.at[k, i]), identity) for k in range(NZ - 1)
        ] + [before_ref[i]]
        while len(factors) > 1:
            factors = [mm(factors[j], factors[j + 1]) for j in range(0, len(factors), 2)]
        out_ref[i] = (factors[0] * SCALE).astype(jnp.bfloat16)
        out_ref[2 + i] = psi_ref[i]


def sources(at_ref):
    own, x, c = at_ref[1], at_ref[4], at_ref[5]
    return [
        lax.rem(x - d + NX, NX) * 2 + (c if same == 0 else 1 - c)
        for d in range(NX)
        for same in range(2)
    ]


def apply_sector(k_ops, phi, left_ref, q, right_ref, p):
    rows = []
    for k in range(k_ops):
        rows.append(
            jnp.dot(left_ref[k, q], phi, preferred_element_type=jnp.float32).astype(jnp.bfloat16)
        )
    half = jnp.concatenate(rows, axis=1)
    right = jnp.concatenate([right_ref[k, p] for k in range(k_ops)], axis=1)
    return lax.dot_general(
        half, right, (((1,), (1,)), ((), ())), preferred_element_type=jnp.float32
    )


def apply_kernel(
    first, k_ops, at_ref, inverse_ref, left_ref, right_ref, *refs
):
    gathered = refs[:8]
    if first:
        keep_ref, send_ref, prefix_ref, prefixes, vectors = refs[8:]
    else:
        keep_ref, send_ref, total_ref, vectors = refs[8:]
    x, c = at_ref[4], at_ref[5]
    total = jnp.zeros((1, N), jnp.float32)
    for source, ref in zip(sources(at_ref), gathered):
        for i in range(2):
            if first:
                prefixes[source * 2 + i] = ref[i]
                vectors[source * 2 + i] = ref[2 + i]
            else:
                vectors[source * 2 + i] = ref[i * N : i * N + N, :]
        if not first:
            total += jnp.sum(ref[2 * N : 2 * N + 16, :].astype(jnp.float32), axis=0, keepdims=True)
    if first:
        for i in range(2):
            prefix_ref[i] = prefixes[inverse_ref[(x * 2 + c) * 2 + i]]
    else:
        total_ref[...] = jnp.broadcast_to(total, (8, N))

    for out_ref, core in ((send_ref, 1 - c), (keep_ref, c)):

        def body(j, carry, out_ref=out_ref, core=core):
            d = j // 2
            i = lax.rem(j, 2)
            p = (lax.rem(x + d, NX) * 2 + core) * 2 + i
            q = inverse_ref[p]
            if first:
                phi = jnp.dot(
                    prefixes[q], vectors[p], preferred_element_type=jnp.float32
                ).astype(jnp.bfloat16)
            else:
                phi = vectors[p]
            out_ref[d, i] = apply_sector(k_ops, phi, left_ref, q, right_ref, p).astype(
                jnp.bfloat16
            )
            return carry

        lax.fori_loop(0, 8, body, 0)


def add_kernel(keep_ref, other_ref, s0, s1, s2, s3):
    for d, ref in enumerate((s0, s1, s2, s3)):
        both = keep_ref[d].astype(jnp.float32) + other_ref[d].astype(jnp.float32)
        ref[...] = both.astype(ref.dtype)


def owner_product(prefix_ref, parts, i):
    total = parts[0][i]
    for part in parts[1:]:
        total += part[i].astype(jnp.float32)
    high = total.astype(jnp.bfloat16)
    low = (total - high.astype(jnp.float32)).astype(jnp.bfloat16)
    dims = (((0,), (0,)), ((), ()))
    prefix = prefix_ref[i]
    return (
        lax.dot_general(prefix, high, dims, preferred_element_type=jnp.float32)
        + lax.dot_general(prefix, low, dims, preferred_element_type=jnp.float32)
    ) * UNSCALE


def middle_kernel(prefix_ref, s0, s1, s2, s3, psi_ref, payload_ref, level_ref):
    blocks = [owner_product(prefix_ref, (s0, s1, s2, s3), i) for i in range(2)]
    squares = jnp.sum(
        blocks[0] * blocks[0] + blocks[1] * blocks[1], axis=(0, 1), keepdims=True
    )
    squares = jnp.broadcast_to(squares, (16, N))
    level = squares[0:1, :] * (1.0 / (2 * N * N)) + 1e-06
    factor = lax.rsqrt(level)
    for i in range(2):
        psi_ref[i] = blocks[i].astype(jnp.bfloat16)
        vector = (blocks[i] * factor).astype(jnp.bfloat16)
        payload_ref[i * N : i * N + N, :] = jnp.dot(
            prefix_ref[i], vector, preferred_element_type=jnp.float32
        ).astype(jnp.bfloat16)
    high = squares.astype(jnp.bfloat16).astype(jnp.float32)
    mid = (squares - high).astype(jnp.bfloat16).astype(jnp.float32)
    low = squares - high - mid
    row = lax.broadcasted_iota(jnp.int32, (16, N), 0)
    parts = jnp.where(row == 0, high, jnp.where(row == 1, mid, jnp.where(row == 2, low, 0.0)))
    payload_ref[2 * N : 2 * N + 16, :] = parts.astype(jnp.bfloat16)
    level_ref[...] = jnp.broadcast_to(level, (8, N))


def last_kernel(prefix_ref, s0, s1, s2, s3, level_ref, total_ref, out_ref):
    overall = lax.rsqrt(total_ref[0:1, :] * (1.0 / (16 * N * N)) + 1e-06)
    ratio = jnp.where(overall > 0.0, overall * jnp.sqrt(level_ref[0:1, :]), 0.0)
    for i in range(2):
        block = owner_product(prefix_ref, (s0, s1, s2, s3), i)
        out_ref[i] = (block * ratio).astype(jnp.bfloat16)


def gather_op(payload):
    mine = [payload] + [lax.ppermute(payload, "x", shift(NX, d)) for d in range(1, NX)]
    out = []
    for part in mine:
        out += [part, lax.ppermute(part, "c", shift(NC, 1))]
    return out


def scatter_sum(keep, send):
    other = lax.ppermute(send, "c", shift(NC, 1))
    block = (2, N, N)
    f32 = jax.ShapeDtypeStruct(block, jnp.float32)
    bf16 = jax.ShapeDtypeStruct(block, jnp.bfloat16)
    sums = call(add_kernel, (f32, bf16, bf16, bf16), [VMEM] * 2, [VMEM] * 4, (keep, other),
                limit=16 << 20)
    return [sums[0]] + [lax.ppermute(sums[d], "x", shift(NX, d)) for d in range(1, NX)]


def on_device(label_map, site_blocks, left_ops, right_ops, wavefunction):
    k_ops = left_ops.shape[0]
    z, y, x, c = (lax.axis_index(a) for a in ("z", "y", "x", "c"))
    at = jnp.stack([z * NY + y, x * 2 + c, y, z, x, c, z, z]).astype(jnp.int32)
    code = jax.ShapeDtypeStruct((2, CODE_ROWS, N), jnp.int16)
    pair = jax.ShapeDtypeStruct((2, N, N), jnp.bfloat16)
    half = jax.ShapeDtypeStruct((NX, 2, N, N), jnp.bfloat16)
    row = jax.ShapeDtypeStruct((8, N), jnp.float32)

    maps = lax.all_to_all(
        jnp.broadcast_to(label_map, (NZ * NY, 16)), SEG, 0, 0, tiled=True
    )
    own_code, inverse = call(
        select_kernel,
        (code, jax.ShapeDtypeStruct((16,), jnp.int32)),
        [SMEM, SMEM, VMEM],
        [VMEM, SMEM],
        (at, maps, site_blocks[0]),
        limit=16 << 20,
    )
    row_codes = [own_code] + [lax.ppermute(own_code, "y", shift(NY, d)) for d in range(1, NY)]
    total_code, before = call(
        row_kernel,
        (
            jax.ShapeDtypeStruct((NZ, 2, CODE_ROWS, N), jnp.int16),
            jax.ShapeDtypeStruct((2, N, N), jnp.float32),
        ),
        [SMEM] + [VMEM] * 4,
        [VMEM] * 2,
        (at, *row_codes),
        [pltpu.VMEM((NY, 2, N, N), jnp.float32)],
        limit=16 << 20,
    )
    codes = lax.all_to_all(total_code, "z", 0, 0, tiled=True)
    payload = call(
        chain_kernel,
        jax.ShapeDtypeStruct((4, N, N), jnp.bfloat16),
        [SMEM] + [VMEM] * 3,
        VMEM,
        (at, codes, before, wavefunction[0]),
        limit=16 << 20,
    )
    flops = 2 * k_ops * 16 * 2 * N * N * N
    limit = 24 << 20
    held = pltpu.VMEM((16, N, N), jnp.bfloat16)
    keep, send, prefix = call(
        functools.partial(apply_kernel, True, k_ops),
        (half, half, pair),
        [SMEM] * 2 + [VMEM] * 10,
        [VMEM] * 3,
        (at, inverse, left_ops, right_ops[0], *gather_op(payload)),
        [held, held],
        flops=flops,
        limit=limit,
    )
    parts = scatter_sum(keep, send)
    first_out, payload, level = call(
        middle_kernel,
        (pair, jax.ShapeDtypeStruct((2 * N + 16, N), jnp.bfloat16), row),
        [VMEM] * 5,
        [VMEM] * 3,
        (prefix, *parts),
        limit=16 << 20,
    )
    keep, send, total = call(
        functools.partial(apply_kernel, False, k_ops),
        (half, half, row),
        [SMEM] * 2 + [VMEM] * 10,
        [VMEM] * 3,
        (at, inverse, left_ops, right_ops[0], *gather_op(payload)),
        [held],
        flops=flops,
        limit=limit,
    )
    parts = scatter_sum(keep, send)
    second_out = call(
        last_kernel, pair, [VMEM] * 7, VMEM, (prefix, *parts, level, total), limit=16 << 20
    )
    return (first_out[None], second_out[None])


def solution(mesh):
    split = Mesh(mesh.devices.reshape(NZ, NY, NX, NC), ("z", "y", "x", "c"))
    placed = (
        P(SEG, None),
        P(SEG, None, None, None),
        P(OP, None, None, None),
        P(SEG, OP, None, None, None),
        P(SEG, OP, None, None),
    )
    return jax.shard_map(
        on_device,
        mesh=split,
        in_specs=placed,
        out_specs=(P(SEG, OP, None, None), P(SEG, OP, None, None)),
        check_vma=False,
    )
```

time: 326 us -> 122 us (0.37); the launches traced: 320 us -> 122 us
  waiting for transfers between devices: 97 us -> 24.1 us
  matrix products: 60.8 us -> 0 us
  blocking collectives: 72.8 us -> 16.9 us
  local copies, waits for them, and re-layouts: 62.6 us -> 9 us
  starting transfers between devices: 5.17 us -> 47.2 us
  Pallas kernels: 0 us -> 24 us
  between operations: 16.2 us -> 0.74 us
  other arithmetic: 5.03 us -> 0 us
    all_gather x2 -> x0, waiting for transfers between devices: 96.3 us -> none  [prefix_by_axis(): pieces = jax.tree.map(lambda part: lax.all_gather(part, axis), running)]
    dot_general x18 -> x0, matrix products: 60.8 us -> none  [the longest x14 25.7 us: compose(): jnp.einsum('qij,qjk->qik', former[0], jnp.take(latter[0], position, axis=...]
    gather x29 -> x0, local copies, waits for them, and re-layouts: 47.7 us -> none  [the longest x14 31.7 us: compose(): jnp.take(latter[0], position, axis=0)]
    ppermute x0 -> x25, starting transfers between devices: none -> 35.2 us  [the longest x8 20 us: gather_op(): out += [part, lax.ppermute(part, 'c', shift(NC, 1))]]
    all_to_all x4 -> x1, blocking collectives: 47.6 us -> 16.9 us  [on_device(): codes = lax.all_to_all(total_code, 'z', 0, 0, tiled=True)]
    pallas_call x0 -> x9, Pallas kernels: none -> 24 us  [call(): pl.pallas_call(kernel, out_shape=outs, in_specs=specs, out_specs=out_spec...]
    unnamed x1 -> x0, blocking collectives: 16.4 us -> none
    ppermute x0 -> x25, waiting for transfers between devices: none -> 15.7 us  [the longest x6 6.73 us: scatter_sum(): lax.ppermute(sums[d], 'x', shift(NX, d))]
  transfers between devices with their start and end apart: 3 -> 26, of which waited for: 2 -> 12; matrix products, arithmetic and copies ran while one was open for 28% -> 0% of each run, Pallas kernels for 0% -> 0%
where the time goes in v1:
time: 122 us
  starting transfers between devices  47.2 us (39%)
  waiting for transfers between devices  24.1 us (20%)
  Pallas kernels  24 us (20%)
  blocking collectives  16.9 us (14%)
  local copies, waits for them, and re-layouts  9 us (7%)
    pallas_call x9, Pallas kernels, call(): pl.pallas_call(kernel, out_shape=outs, in_specs=specs, out_specs=out_spec...  24 us
    ppermute x8, starting transfers between devices, gather_op(): out += [part, lax.ppermute(part, 'c', shift(NC, 1))]  20 us
    all_to_all x1, blocking collectives, on_device(): codes = lax.all_to_all(total_code, 'z', 0, 0, tiled=True)  16.9 us
    all_to_all x1, starting transfers between devices, on_device(): lax.all_to_all(jnp.broadcast_to(label_map, (NZ * NY, 16)), SEG, 0, 0, til...  12 us
    all_to_all x1, waiting for transfers between devices, on_device(): lax.all_to_all(jnp.broadcast_to(label_map, (NZ * NY, 16)), SEG, 0, 0, til...  8.44 us
    unnamed x12, local copies, waits for them, and re-layouts  7.64 us
    ppermute x6, waiting for transfers between devices, scatter_sum(): lax.ppermute(sums[d], 'x', shift(NX, d))  6.73 us
    ppermute x6, starting transfers between devices, gather_op(): lax.ppermute(payload, 'x', shift(NX, d))  6.24 us
  transfers between devices with their start and end apart: 26, of which 12 were waited for; matrix products, arithmetic and copies ran while one was open for 0% of the time, Pallas kernels for 0%

profile of v1, /device:TPU:1, one launch (start us, length us, event | category | flops | bytes accessed | tf_op | source)
XLA Modules:
  0.0 122.0 jit_solution(11354430371745289571)
XLA Ops:
  0.6 1.3 %broadcast_in_dim.11 = s32[32,1,16]{2,1,0:T(1,128)} broadcast(s32[16]{0:T(128)} %bitcast.19), dimensions={2} | broadcast | bytes 2112 | tf_op jit(solution)/shard_map/broadcast_in_dim | solution.py:262
  1.9 12.0 %all-to-all-start = ((s32[32,1,16]{2,1,0:T(1,128)}), s32[32,1,16]{2,1,0:T(1,128)S(1)}, u32[]{:S(2)}, u32[]{:S(2)}) async-start(s32[32,1,16]{2,1,0:T(1,128)} %broadcast_in_dim.11), calls=%async_computation | async-start | bytes 32768 | tf_op jit(solution)/shard_map/all_to_all | solution.py:261
  14.0 8.4 %all-to-all-done = s32[32,1,16]{2,1,0:T(1,128)S(1)} async-done(((s32[32,1,16]{2,1,0:T(1,128)}), s32[32,1,16]{2,1,0:T(1,128)S(1)}, u32[]{:S(2)}, u32[]{:S(2)}) %all-to-all-start) | async-done | bytes 2080 | tf_op jit(solution)/shard_map/all_to_all | solution.py:261
  22.5 1.2 %copy-done.4 = f32[1,16,128,128]{3,2,1,0:T(8,128)S(1)} copy-done((f32[1,16,128,128]{3,2,1,0:T(8,128)S(1)}, f32[1,16,128,128]{3,2,1,0:T(8,128)}, u32[]{:S(2)}) %copy-start.4) | copy-done | bytes 1048600
  23.7 1.5 %shard_map.71 = (s16[2,144,128]{2,1,0:T(8,128)(2,1)S(1)}, s32[16]{0:T(128)S(1)}) custom-call(s32[8]{0:T(128)S(1)} %stack.29.at_ref, s32[32,16]{1,0:T(8,128)S(1)} %bitcast.16, f32[16,128,128]{2,1,0:T(8,128)S(1)} %bitcast.15), custom_call_target="tpu_custom_call" | custom-call | bytes 1048576 | tf_op jit(solution)/shard_map/pallas_call | solution.py:29
  25.1 1.1 collective-permute-start.2
  27.4 1.1 collective-permute-done.2.s3
  28.4 2.6 %collective-permute-done.1.s2 = s16[2,144,128]{2,1,0:T(8,128)(2,1)S(1)} collective-permute-done((s16[2,144,128]{2,1,0:T(8,128)(2,1)S(1)}, s16[2,144,128]{2,1,0:T(8,128)(2,1)S(1)}, u32[]{:S(2)}, u32[]{:S(2)}) %collective-permute-start.1) | collective-permute-done | bytes 73760 | tf_op jit(solution)/shard_map/ppermute | solution.py:272
  31.8 1.5 %shard_map.72 = (s16[8,2,144,128]{3,2,1,0:T(8,128)(2,1)S(1)}, f32[2,128,128]{2,1,0:T(8,128)S(1)}) custom-call(s32[8]{0:T(128)S(1)} %stack.29.at_ref, s16[2,144,128]{2,1,0:T(8,128)(2,1)S(1)} %get-tuple-element.24.s0, s16[2,144,128]{2,1,0:T(8,128)(2,1)S(1)} %collective-permute-done.s1, s16[2,144,128]{2,1,0:T(8,128)(2,1)S(1)} %collective-permute-done.1.s2, ...), custom_call_target="tpu_custom_call" | custom-call | bytes 1048576 | tf_op jit(solution)/shard_map/pallas_call | solution.py:29
  33.3 16.9 %all_to_all.13.codes_ref = s16[8,2,144,128]{3,2,1,0:T(8,128)(2,1)S(1)} all-to-all(s16[8,2,144,128]{3,2,1,0:T(8,128)(2,1)S(1)} %get-tuple-element.25), channel_id=1, replica_groups=mesh['z'=8,'y'=4,'x'=4,'c'=2] {'z'}, dimensions={0} | all-to-all | bytes 1179648 | tf_op jit(solution)/shard_map/all_to_all | solution.py:285
  51.0 2.1 %shard_map.73.refs_0_ = bf16[4,128,128]{2,1,0:T(8,128)(2,1)S(1)} custom-call(s32[8]{0:T(128)S(1)} %stack.29.at_ref, s16[8,2,144,128]{3,2,1,0:T(8,128)(2,1)S(1)} %all_to_all.13.codes_ref, f32[2,128,128]{2,1,0:T(8,128)S(1)} %get-tuple-element.26.before_ref, bf16[2,128,128]{2,1,0:T(8,128)(2,1)S(1)} %bitcast.17), custom_call_target="tpu_custom_call" | custom-call | bytes 1048576 | tf_op jit(solution)/shard_map/pallas_call | solution.py:29
  53.1 2.6 %collective-permute-start.8 = (bf16[4,128,128]{2,1,0:T(8,128)(2,1)S(1)}, bf16[4,128,128]{2,1,0:T(8,128)(2,1)S(1)}, u32[]{:S(2)}, u32[]{:S(2)}) collective-permute-start(bf16[4,128,128]{2,1,0:T(8,128)(2,1)S(1)} %shard_map.73.refs_0_), channel_id=1, source_target_pairs={{0,6},{2,0},{4,2},{6,4},{1,7},{3,1},{5,3},{7,5},{8,14},{10,8},{12,... | collective-permute-start | bytes 393224 | tf_op jit(solution)/shard_map/ppermute | solution.py:235
  56.8 6.2 %collective-permute-start.3 = (bf16[4,128,128]{2,1,0:T(8,128)(2,1)S(1)}, bf16[4,128,128]{2,1,0:T(8,128)(2,1)S(1)}, u32[]{:S(2)}, u32[]{:S(2)}) collective-permute-start(bf16[4,128,128]{2,1,0:T(8,128)(2,1)S(1)} %shard_map.73.refs_0_), channel_id=1, source_target_pairs={{0,1},{1,0},{2,3},{3,2},{4,5},{5,4},{6,7},{7,6},{8,9},{9,8},{10,11... | collective-permute-start | bytes 393224 | tf_op jit(solution)/shard_map/ppermute | solution.py:238
  63.0 2.2 %collective-permute-start.9 = (bf16[4,128,128]{2,1,0:T(8,128)(2,1)S(1)}, bf16[4,128,128]{2,1,0:T(8,128)(2,1)S(1)}, u32[]{:S(2)}, u32[]{:S(2)}) collective-permute-start(bf16[4,128,128]{2,1,0:T(8,128)(2,1)S(1)} %collective-permute-done.8.refs_6_), channel_id=1, source_target_pairs={{0,1},{1,0},{2,3},{3,2},{4,5},{5,4},{6,7},{7,6},{8,9},{9,8},{10,11... | collective-permute-start | bytes 393224 | tf_op jit(solution)/shard_map/ppermute | solution.py:238
  65.3 2.6 %collective-permute-start.7 = (bf16[4,128,128]{2,1,0:T(8,128)(2,1)S(1)}, bf16[4,128,128]{2,1,0:T(8,128)(2,1)S(1)}, u32[]{:S(2)}, u32[]{:S(2)}) collective-permute-start(bf16[4,128,128]{2,1,0:T(8,128)(2,1)S(1)} %collective-permute-done.6.refs_4_), channel_id=1, source_target_pairs={{0,1},{1,0},{2,3},{3,2},{4,5},{5,4},{6,7},{7,6},{8,9},{9,8},{10,11... | collective-permute-start | bytes 393224 | tf_op jit(solution)/shard_map/ppermute | solution.py:238
  67.9 1.3 %collective-permute-start.5 = (bf16[4,128,128]{2,1,0:T(8,128)(2,1)S(1)}, bf16[4,128,128]{2,1,0:T(8,128)(2,1)S(1)}, u32[]{:S(2)}, u32[]{:S(2)}) collective-permute-start(bf16[4,128,128]{2,1,0:T(8,128)(2,1)S(1)} %collective-permute-done.4.refs_2_), channel_id=1, source_target_pairs={{0,1},{1,0},{2,3},{3,2},{4,5},{5,4},{6,7},{7,6},{8,9},{9,8},{10,11... | collective-permute-start | bytes 393224 | tf_op jit(solution)/shard_map/ppermute | solution.py:238
  70.2 2.8 %copy-done = bf16[12,16,128,128]{3,2,1,0:T(8,128)(2,1)S(1)} copy-done((bf16[12,16,128,128]{3,2,1,0:T(8,128)(2,1)S(1)}, bf16[12,16,128,128]{3,2,1,0:T(8,128)(2,1)}, u32[]{:S(2)}) %copy-start) | copy-done | bytes 6291480
  73.0 2.8 %copy-done.2 = bf16[1,12,16,128,128]{4,3,2,1,0:T(8,128)(2,1)S(1)} copy-done((bf16[1,12,16,128,128]{4,3,2,1,0:T(8,128)(2,1)S(1)}, bf16[1,12,16,128,128]{4,3,2,1,0:T(8,128)(2,1)}, u32[]{:S(2)}) %copy-start.2) | copy-done | bytes 6291480
  75.8 9.6 %shard_map.74 = (bf16[4,2,128,128]{3,2,1,0:T(8,128)(2,1)S(1)}, bf16[4,2,128,128]{3,2,1,0:T(8,128)(2,1)S(1)}, bf16[2,128,128]{2,1,0:T(8,128)(2,1)S(1)}) custom-call(s32[8]{0:T(128)S(1)} %stack.29.at_ref, s32[16]{0:T(128)S(1)} %get-tuple-element.23.inverse_ref, bf16[12,16,128,128]{3,2,1,0:T(8,128)(2,1)S(1)} %copy-done, ...), custom_call_target="tpu_custom_call" | custom-call | flops 1610612736 | bytes 1048576 | tf_op jit(solution)/shard_map/pallas_call | solution.py:29
  85.8 1.2 collective-permute-done.10.other_ref
  87.1 1.5 %collective-permute-start.12 = (bf16[2,128,128]{2,1,0:T(8,128)(2,1)S(1)}, bf16[2,128,128]{2,1,0:T(8,128)(2,1)S(1)}, u32[]{:S(2)}, u32[]{:S(2)}) collective-permute-start(bf16[2,128,128]{2,1,0:T(8,128)(2,1)S(1)} %get-tuple-element.32), channel_id=1, source_target_pairs={{0,4},{2,6},{4,0},{6,2},{1,5},{3,7},{5,1},{7,3},{8,12},{10,14},{12... | collective-permute-start | bytes 196616 | tf_op jit(solution)/shard_map/ppermute | solution.py:249
  88.6 1.2 collective-permute-start.13
  89.8 3.6 %collective-permute-done.11.s1 = bf16[2,128,128]{2,1,0:T(8,128)(2,1)S(1)} collective-permute-done((bf16[2,128,128]{2,1,0:T(8,128)(2,1)S(1)}, bf16[2,128,128]{2,1,0:T(8,128)(2,1)S(1)}, u32[]{:S(2)}, u32[]{:S(2)}) %collective-permute-start.11) | collective-permute-done | bytes 65568 | tf_op jit(solution)/shard_map/ppermute | solution.py:249
  94.2 2.0 %collective-permute-start.19 = (bf16[272,128]{1,0:T(8,128)(2,1)S(1)}, bf16[272,128]{1,0:T(8,128)(2,1)S(1)}, u32[]{:S(2)}, u32[]{:S(2)}) collective-permute-start(bf16[272,128]{1,0:T(8,128)(2,1)S(1)} %get-tuple-element.35.refs_0_), channel_id=1, source_target_pairs={{0,6},{2,0},{4,2},{6,4},{1,7},{3,1},{5,3},{7,5},{8,14},{10,8},{12,... | collective-permute-start | bytes 208904 | tf_op jit(solution)/shard_map/ppermute | solution.py:235
  96.8 2.1 %collective-permute-start.14 = (bf16[272,128]{1,0:T(8,128)(2,1)S(1)}, bf16[272,128]{1,0:T(8,128)(2,1)S(1)}, u32[]{:S(2)}, u32[]{:S(2)}) collective-permute-start(bf16[272,128]{1,0:T(8,128)(2,1)S(1)} %get-tuple-element.35.refs_0_), channel_id=1, source_target_pairs={{0,1},{1,0},{2,3},{3,2},{4,5},{5,4},{6,7},{7,6},{8,9},{9,8},{10,11... | collective-permute-start | bytes 208904 | tf_op jit(solution)/shard_map/ppermute | solution.py:238
  98.9 1.7 %collective-permute-start.20 = (bf16[272,128]{1,0:T(8,128)(2,1)S(1)}, bf16[272,128]{1,0:T(8,128)(2,1)S(1)}, u32[]{:S(2)}, u32[]{:S(2)}) collective-permute-start(bf16[272,128]{1,0:T(8,128)(2,1)S(1)} %collective-permute-done.19.refs_6_), channel_id=1, source_target_pairs={{0,1},{1,0},{2,3},{3,2},{4,5},{5,4},{6,7},{7,6},{8,9},{9,8},{10,11... | collective-permute-start | bytes 208904 | tf_op jit(solution)/shard_map/ppermute | solution.py:238
  100.9 3.0 %collective-permute-start.18 = (bf16[272,128]{1,0:T(8,128)(2,1)S(1)}, bf16[272,128]{1,0:T(8,128)(2,1)S(1)}, u32[]{:S(2)}, u32[]{:S(2)}) collective-permute-start(bf16[272,128]{1,0:T(8,128)(2,1)S(1)} %collective-permute-done.17.refs_4_), channel_id=1, source_target_pairs={{0,1},{1,0},{2,3},{3,2},{4,5},{5,4},{6,7},{7,6},{8,9},{9,8},{10,11... | collective-permute-start | bytes 208904 | tf_op jit(solution)/shard_map/ppermute | solution.py:238
  105.5 7.6 %shard_map.77 = (bf16[4,2,128,128]{3,2,1,0:T(8,128)(2,1)S(1)}, bf16[4,2,128,128]{3,2,1,0:T(8,128)(2,1)S(1)}, f32[8,128]{1,0:T(8,128)S(1)}) custom-call(s32[8]{0:T(128)S(1)} %stack.29.at_ref, s32[16]{0:T(128)S(1)} %get-tuple-element.23.inverse_ref, bf16[12,16,128,128]{3,2,1,0:T(8,128)(2,1)S(1)} %copy-done.1, bf16[12,16,128,128]{3,2,1,0:T(8,128)(2,1)S(1)} %bitcast.14, ...), custom_call_target="tpu_custom_call" | custom-call | flops 1610612736 | bytes 1048576 | tf_op jit(solution)/shard_map/pallas_call | solution.py:29
  113.6 1.2 collective-permute-done.21.other_ref
  114.9 1.5 %collective-permute-start.23 = (bf16[2,128,128]{2,1,0:T(8,128)(2,1)S(1)}, bf16[2,128,128]{2,1,0:T(8,128)(2,1)S(1)}, u32[]{:S(2)}, u32[]{:S(2)}) collective-permute-start(bf16[2,128,128]{2,1,0:T(8,128)(2,1)S(1)} %get-tuple-element.40), channel_id=1, source_target_pairs={{0,4},{2,6},{4,0},{6,2},{1,5},{3,7},{5,1},{7,3},{8,12},{10,14},{12... | collective-permute-start | bytes 196616 | tf_op jit(solution)/shard_map/ppermute | solution.py:249
  116.4 1.6 %collective-permute-start.24 = (bf16[2,128,128]{2,1,0:T(8,128)(2,1)S(1)}, bf16[2,128,128]{2,1,0:T(8,128)(2,1)S(1)}, u32[]{:S(2)}, u32[]{:S(2)}) collective-permute-start(bf16[2,128,128]{2,1,0:T(8,128)(2,1)S(1)} %get-tuple-element.41), channel_id=1, source_target_pairs={{0,6},{2,0},{4,2},{6,4},{1,7},{3,1},{5,3},{7,5},{8,14},{10,8},{12,... | collective-permute-start | bytes 196616 | tf_op jit(solution)/shard_map/ppermute | solution.py:249
  118.0 3.2 %collective-permute-done.22.s1 = bf16[2,128,128]{2,1,0:T(8,128)(2,1)S(1)} collective-permute-done((bf16[2,128,128]{2,1,0:T(8,128)(2,1)S(1)}, bf16[2,128,128]{2,1,0:T(8,128)(2,1)S(1)}, u32[]{:S(2)}, u32[]{:S(2)}) %collective-permute-start.22) | collective-permute-done | bytes 65568 | tf_op jit(solution)/shard_map/ppermute | solution.py:249
  (44 shorter events, 10.3 us)
Async XLA Ops:
  1.9 20.6 %all-to-all-start = ((s32[32,1,16]{2,1,0:T(1,128)}), s32[32,1,16]{2,1,0:T(1,128)S(1)}, u32[]{:S(2)}, u32[]{:S(2)}) async-start(s32[32,1,16]{2,1,0:T(1,128)} %broadcast_in_dim.11), calls=%async_computation | async-start | bytes 32768 | tf_op jit(solution)/shard_map/all_to_all | solution.py:261
  22.5 1.2 %copy-start.4 = (f32[1,16,128,128]{3,2,1,0:T(8,128)S(1)}, f32[1,16,128,128]{3,2,1,0:T(8,128)}, u32[]{:S(2)}) copy-start(f32[1,16,128,128]{3,2,1,0:T(8,128)} %param.6) | copy-start | bytes 3145732
  25.1 3.3 %collective-permute-start.2 = (s16[2,144,128]{2,1,0:T(8,128)(2,1)S(1)}, s16[2,144,128]{2,1,0:T(8,128)(2,1)S(1)}, u32[]{:S(2)}, u32[]{:S(2)}) collective-permute-start(s16[2,144,128]{2,1,0:T(8,128)(2,1)S(1)} %get-tuple-element.24.s0), channel_id=1, source_target_pairs={{0,24},{8,0},{16,8},{24,16},{1,25},{9,1},{17,9},{25,17},{2,26},{10... | collective-permute-start | bytes 221192 | tf_op jit(solution)/shard_map/ppermute | solution.py:272
  26.3 4.7 %collective-permute-start.1 = (s16[2,144,128]{2,1,0:T(8,128)(2,1)S(1)}, s16[2,144,128]{2,1,0:T(8,128)(2,1)S(1)}, u32[]{:S(2)}, u32[]{:S(2)}) collective-permute-start(s16[2,144,128]{2,1,0:T(8,128)(2,1)S(1)} %get-tuple-element.24.s0), channel_id=1, source_target_pairs={{0,16},{8,24},{16,0},{24,8},{1,17},{9,25},{17,1},{25,9},{2,18},{10... | collective-permute-start | bytes 221192 | tf_op jit(solution)/shard_map/ppermute | solution.py:272
  27.4 4.4 %collective-permute-start = (s16[2,144,128]{2,1,0:T(8,128)(2,1)S(1)}, s16[2,144,128]{2,1,0:T(8,128)(2,1)S(1)}, u32[]{:S(2)}, u32[]{:S(2)}) collective-permute-start(s16[2,144,128]{2,1,0:T(8,128)(2,1)S(1)} %get-tuple-element.24.s0), channel_id=1, source_target_pairs={{0,8},{8,16},{16,24},{24,0},{1,9},{9,17},{17,25},{25,1},{2,10},{10... | collective-permute-start | bytes 221192 | tf_op jit(solution)/shard_map/ppermute | solution.py:272
  50.2 0.8 copy-start.5
  53.1 9.9 %collective-permute-start.8 = (bf16[4,128,128]{2,1,0:T(8,128)(2,1)S(1)}, bf16[4,128,128]{2,1,0:T(8,128)(2,1)S(1)}, u32[]{:S(2)}, u32[]{:S(2)}) collective-permute-start(bf16[4,128,128]{2,1,0:T(8,128)(2,1)S(1)} %shard_map.73.refs_0_), channel_id=1, source_target_pairs={{0,6},{2,0},{4,2},{6,4},{1,7},{3,1},{5,3},{7,5},{8,14},{10,8},{12,... | collective-permute-start | bytes 393224 | tf_op jit(solution)/shard_map/ppermute | solution.py:235
  55.7 9.6 %collective-permute-start.6 = (bf16[4,128,128]{2,1,0:T(8,128)(2,1)S(1)}, bf16[4,128,128]{2,1,0:T(8,128)(2,1)S(1)}, u32[]{:S(2)}, u32[]{:S(2)}) collective-permute-start(bf16[4,128,128]{2,1,0:T(8,128)(2,1)S(1)} %shard_map.73.refs_0_), channel_id=1, source_target_pairs={{0,4},{2,6},{4,0},{6,2},{1,5},{3,7},{5,1},{7,3},{8,12},{10,14},{12... | collective-permute-start | bytes 393224 | tf_op jit(solution)/shard_map/ppermute | solution.py:235
  56.2 11.7 %collective-permute-start.4 = (bf16[4,128,128]{2,1,0:T(8,128)(2,1)S(1)}, bf16[4,128,128]{2,1,0:T(8,128)(2,1)S(1)}, u32[]{:S(2)}, u32[]{:S(2)}) collective-permute-start(bf16[4,128,128]{2,1,0:T(8,128)(2,1)S(1)} %shard_map.73.refs_0_), channel_id=1, source_target_pairs={{0,2},{2,4},{4,6},{6,0},{1,3},{3,5},{5,7},{7,1},{8,10},{10,12},{12... | collective-permute-start | bytes 393224 | tf_op jit(solution)/shard_map/ppermute | solution.py:235
  56.8 12.4 %collective-permute-start.3 = (bf16[4,128,128]{2,1,0:T(8,128)(2,1)S(1)}, bf16[4,128,128]{2,1,0:T(8,128)(2,1)S(1)}, u32[]{:S(2)}, u32[]{:S(2)}) collective-permute-start(bf16[4,128,128]{2,1,0:T(8,128)(2,1)S(1)} %shard_map.73.refs_0_), channel_id=1, source_target_pairs={{0,1},{1,0},{2,3},{3,2},{4,5},{5,4},{6,7},{7,6},{8,9},{9,8},{10,11... | collective-permute-start | bytes 393224 | tf_op jit(solution)/shard_map/ppermute | solution.py:238
  63.0 6.2 %collective-permute-start.9 = (bf16[4,128,128]{2,1,0:T(8,128)(2,1)S(1)}, bf16[4,128,128]{2,1,0:T(8,128)(2,1)S(1)}, u32[]{:S(2)}, u32[]{:S(2)}) collective-permute-start(bf16[4,128,128]{2,1,0:T(8,128)(2,1)S(1)} %collective-permute-done.8.refs_6_), channel_id=1, source_target_pairs={{0,1},{1,0},{2,3},{3,2},{4,5},{5,4},{6,7},{7,6},{8,9},{9,8},{10,11... | collective-permute-start | bytes 393224 | tf_op jit(solution)/shard_map/ppermute | solution.py:238
  65.3 4.0 %collective-permute-start.7 = (bf16[4,128,128]{2,1,0:T(8,128)(2,1)S(1)}, bf16[4,128,128]{2,1,0:T(8,128)(2,1)S(1)}, u32[]{:S(2)}, u32[]{:S(2)}) collective-permute-start(bf16[4,128,128]{2,1,0:T(8,128)(2,1)S(1)} %collective-permute-done.6.refs_4_), channel_id=1, source_target_pairs={{0,1},{1,0},{2,3},{3,2},{4,5},{5,4},{6,7},{7,6},{8,9},{9,8},{10,11... | collective-permute-start | bytes 393224 | tf_op jit(solution)/shard_map/ppermute | solution.py:238
  67.9 2.3 %collective-permute-start.5 = (bf16[4,128,128]{2,1,0:T(8,128)(2,1)S(1)}, bf16[4,128,128]{2,1,0:T(8,128)(2,1)S(1)}, u32[]{:S(2)}, u32[]{:S(2)}) collective-permute-start(bf16[4,128,128]{2,1,0:T(8,128)(2,1)S(1)} %collective-permute-done.4.refs_2_), channel_id=1, source_target_pairs={{0,1},{1,0},{2,3},{3,2},{4,5},{5,4},{6,7},{7,6},{8,9},{9,8},{10,11... | collective-permute-start | bytes 393224 | tf_op jit(solution)/shard_map/ppermute | solution.py:238
  70.2 2.8 %copy-start = (bf16[12,16,128,128]{3,2,1,0:T(8,128)(2,1)S(1)}, bf16[12,16,128,128]{3,2,1,0:T(8,128)(2,1)}, u32[]{:S(2)}) copy-start(bf16[12,16,128,128]{3,2,1,0:T(8,128)(2,1)} %left_ref.3) | copy-start | bytes 18874372
  73.0 2.8 %copy-start.2 = (bf16[1,12,16,128,128]{4,3,2,1,0:T(8,128)(2,1)S(1)}, bf16[1,12,16,128,128]{4,3,2,1,0:T(8,128)(2,1)}, u32[]{:S(2)}) copy-start(bf16[1,12,16,128,128]{4,3,2,1,0:T(8,128)(2,1)} %param.8) | copy-start | bytes 18874372
  75.8 29.7 %copy-start.1 = (bf16[12,16,128,128]{3,2,1,0:T(8,128)(2,1)S(1)}, bf16[12,16,128,128]{3,2,1,0:T(8,128)(2,1)}, u32[]{:S(2)}) copy-start(bf16[12,16,128,128]{3,2,1,0:T(8,128)(2,1)} %left_ref.3) | copy-start | bytes 18874372
  75.8 29.7 %copy-start.3 = (bf16[1,12,16,128,128]{4,3,2,1,0:T(8,128)(2,1)S(1)}, bf16[1,12,16,128,128]{4,3,2,1,0:T(8,128)(2,1)}, u32[]{:S(2)}) copy-start(bf16[1,12,16,128,128]{4,3,2,1,0:T(8,128)(2,1)} %param.8) | copy-start | bytes 18874372
  85.3 1.6 %collective-permute-start.10 = (bf16[4,2,128,128]{3,2,1,0:T(8,128)(2,1)S(1)}, bf16[4,2,128,128]{3,2,1,0:T(8,128)(2,1)S(1)}, u32[]{:S(2)}, u32[]{:S(2)}) collective-permute-start(bf16[4,2,128,128]{3,2,1,0:T(8,128)(2,1)S(1)} %get-tuple-element.29), channel_id=1, source_target_pairs={{0,1},{1,0},{2,3},{3,2},{4,5},{5,4},{6,7},{7,6},{8,9},{9,8},{10,11... | collective-permute-start | bytes 786440 | tf_op jit(solution)/shard_map/ppermute | solution.py:243
  87.0 6.3 %collective-permute-start.11 = (bf16[2,128,128]{2,1,0:T(8,128)(2,1)S(1)}, bf16[2,128,128]{2,1,0:T(8,128)(2,1)S(1)}, u32[]{:S(2)}, u32[]{:S(2)}) collective-permute-start(bf16[2,128,128]{2,1,0:T(8,128)(2,1)S(1)} %get-tuple-element.31), channel_id=1, source_target_pairs={{0,2},{2,4},{4,6},{6,0},{1,3},{3,5},{5,7},{7,1},{8,10},{10,12},{12... | collective-permute-start | bytes 196616 | tf_op jit(solution)/shard_map/ppermute | solution.py:249
  87.1 6.2 %collective-permute-start.12 = (bf16[2,128,128]{2,1,0:T(8,128)(2,1)S(1)}, bf16[2,128,128]{2,1,0:T(8,128)(2,1)S(1)}, u32[]{:S(2)}, u32[]{:S(2)}) collective-permute-start(bf16[2,128,128]{2,1,0:T(8,128)(2,1)S(1)} %get-tuple-element.32), channel_id=1, source_target_pairs={{0,4},{2,6},{4,0},{6,2},{1,5},{3,7},{5,1},{7,3},{8,12},{10,14},{12... | collective-permute-start | bytes 196616 | tf_op jit(solution)/shard_map/ppermute | solution.py:249
  88.6 4.8 %collective-permute-start.13 = (bf16[2,128,128]{2,1,0:T(8,128)(2,1)S(1)}, bf16[2,128,128]{2,1,0:T(8,128)(2,1)S(1)}, u32[]{:S(2)}, u32[]{:S(2)}) collective-permute-start(bf16[2,128,128]{2,1,0:T(8,128)(2,1)S(1)} %get-tuple-element.33), channel_id=1, source_target_pairs={{0,6},{2,0},{4,2},{6,4},{1,7},{3,1},{5,3},{7,5},{8,14},{10,8},{12,... | collective-permute-start | bytes 196616 | tf_op jit(solution)/shard_map/ppermute | solution.py:249
  94.2 4.7 %collective-permute-start.19 = (bf16[272,128]{1,0:T(8,128)(2,1)S(1)}, bf16[272,128]{1,0:T(8,128)(2,1)S(1)}, u32[]{:S(2)}, u32[]{:S(2)}) collective-permute-start(bf16[272,128]{1,0:T(8,128)(2,1)S(1)} %get-tuple-element.35.refs_0_), channel_id=1, source_target_pairs={{0,6},{2,0},{4,2},{6,4},{1,7},{3,1},{5,3},{7,5},{8,14},{10,8},{12,... | collective-permute-start | bytes 208904 | tf_op jit(solution)/shard_map/ppermute | solution.py:235
  96.2 4.7 %collective-permute-start.17 = (bf16[272,128]{1,0:T(8,128)(2,1)S(1)}, bf16[272,128]{1,0:T(8,128)(2,1)S(1)}, u32[]{:S(2)}, u32[]{:S(2)}) collective-permute-start(bf16[272,128]{1,0:T(8,128)(2,1)S(1)} %get-tuple-element.35.refs_0_), channel_id=1, source_target_pairs={{0,4},{2,6},{4,0},{6,2},{1,5},{3,7},{5,1},{7,3},{8,12},{10,14},{12... | collective-permute-start | bytes 208904 | tf_op jit(solution)/shard_map/ppermute | solution.py:235
  96.6 7.3 %collective-permute-start.15 = (bf16[272,128]{1,0:T(8,128)(2,1)S(1)}, bf16[272,128]{1,0:T(8,128)(2,1)S(1)}, u32[]{:S(2)}, u32[]{:S(2)}) collective-permute-start(bf16[272,128]{1,0:T(8,128)(2,1)S(1)} %get-tuple-element.35.refs_0_), channel_id=1, source_target_pairs={{0,2},{2,4},{4,6},{6,0},{1,3},{3,5},{5,7},{7,1},{8,10},{10,12},{12... | collective-permute-start | bytes 208904 | tf_op jit(solution)/shard_map/ppermute | solution.py:235
  96.8 7.8 %collective-permute-start.14 = (bf16[272,128]{1,0:T(8,128)(2,1)S(1)}, bf16[272,128]{1,0:T(8,128)(2,1)S(1)}, u32[]{:S(2)}, u32[]{:S(2)}) collective-permute-start(bf16[272,128]{1,0:T(8,128)(2,1)S(1)} %get-tuple-element.35.refs_0_), channel_id=1, source_target_pairs={{0,1},{1,0},{2,3},{3,2},{4,5},{5,4},{6,7},{7,6},{8,9},{9,8},{10,11... | collective-permute-start | bytes 208904 | tf_op jit(solution)/shard_map/ppermute | solution.py:238
  98.9 5.7 %collective-permute-start.20 = (bf16[272,128]{1,0:T(8,128)(2,1)S(1)}, bf16[272,128]{1,0:T(8,128)(2,1)S(1)}, u32[]{:S(2)}, u32[]{:S(2)}) collective-permute-start(bf16[272,128]{1,0:T(8,128)(2,1)S(1)} %collective-permute-done.19.refs_6_), channel_id=1, source_target_pairs={{0,1},{1,0},{2,3},{3,2},{4,5},{5,4},{6,7},{7,6},{8,9},{9,8},{10,11... | collective-permute-start | bytes 208904 | tf_op jit(solution)/shard_map/ppermute | solution.py:238
  100.9 3.9 %collective-permute-start.18 = (bf16[272,128]{1,0:T(8,128)(2,1)S(1)}, bf16[272,128]{1,0:T(8,128)(2,1)S(1)}, u32[]{:S(2)}, u32[]{:S(2)}) collective-permute-start(bf16[272,128]{1,0:T(8,128)(2,1)S(1)} %collective-permute-done.17.refs_4_), channel_id=1, source_target_pairs={{0,1},{1,0},{2,3},{3,2},{4,5},{5,4},{6,7},{7,6},{8,9},{9,8},{10,11... | collective-permute-start | bytes 208904 | tf_op jit(solution)/shard_map/ppermute | solution.py:238
  103.9 1.6 %collective-permute-start.16 = (bf16[272,128]{1,0:T(8,128)(2,1)S(1)}, bf16[272,128]{1,0:T(8,128)(2,1)S(1)}, u32[]{:S(2)}, u32[]{:S(2)}) collective-permute-start(bf16[272,128]{1,0:T(8,128)(2,1)S(1)} %collective-permute-done.15.refs_2_), channel_id=1, source_target_pairs={{0,1},{1,0},{2,3},{3,2},{4,5},{5,4},{6,7},{7,6},{8,9},{9,8},{10,11... | collective-permute-start | bytes 208904 | tf_op jit(solution)/shard_map/ppermute | solution.py:238
  113.1 1.6 %collective-permute-start.21 = (bf16[4,2,128,128]{3,2,1,0:T(8,128)(2,1)S(1)}, bf16[4,2,128,128]{3,2,1,0:T(8,128)(2,1)S(1)}, u32[]{:S(2)}, u32[]{:S(2)}) collective-permute-start(bf16[4,2,128,128]{3,2,1,0:T(8,128)(2,1)S(1)} %get-tuple-element.37), channel_id=1, source_target_pairs={{0,1},{1,0},{2,3},{3,2},{4,5},{5,4},{6,7},{7,6},{8,9},{9,8},{10,11... | collective-permute-start | bytes 786440 | tf_op jit(solution)/shard_map/ppermute | solution.py:243
  114.8 6.3 %collective-permute-start.22 = (bf16[2,128,128]{2,1,0:T(8,128)(2,1)S(1)}, bf16[2,128,128]{2,1,0:T(8,128)(2,1)S(1)}, u32[]{:S(2)}, u32[]{:S(2)}) collective-permute-start(bf16[2,128,128]{2,1,0:T(8,128)(2,1)S(1)} %get-tuple-element.39), channel_id=1, source_target_pairs={{0,2},{2,4},{4,6},{6,0},{1,3},{3,5},{5,7},{7,1},{8,10},{10,12},{12... | collective-permute-start | bytes 196616 | tf_op jit(solution)/shard_map/ppermute | solution.py:249
  114.9 6.2 %collective-permute-start.23 = (bf16[2,128,128]{2,1,0:T(8,128)(2,1)S(1)}, bf16[2,128,128]{2,1,0:T(8,128)(2,1)S(1)}, u32[]{:S(2)}, u32[]{:S(2)}) collective-permute-start(bf16[2,128,128]{2,1,0:T(8,128)(2,1)S(1)} %get-tuple-element.40), channel_id=1, source_target_pairs={{0,4},{2,6},{4,0},{6,2},{1,5},{3,7},{5,1},{7,3},{8,12},{10,14},{12... | collective-permute-start | bytes 196616 | tf_op jit(solution)/shard_map/ppermute | solution.py:249
  116.4 4.8 %collective-permute-start.24 = (bf16[2,128,128]{2,1,0:T(8,128)(2,1)S(1)}, bf16[2,128,128]{2,1,0:T(8,128)(2,1)S(1)}, u32[]{:S(2)}, u32[]{:S(2)}) collective-permute-start(bf16[2,128,128]{2,1,0:T(8,128)(2,1)S(1)} %get-tuple-element.41), channel_id=1, source_target_pairs={{0,6},{2,0},{4,2},{6,4},{1,7},{3,1},{5,3},{7,5},{8,14},{10,8},{12,... | collective-permute-start | bytes 196616 | tf_op jit(solution)/shard_map/ppermute | solution.py:249
